TPU v7x, 256 devices: a whole 4x4x8 slice. The times are simulated.
256 devices in a mesh: rows: 32 (over z_hi, y, core), cols: 8 (over x, z_lo).
Axes of the slice: x: 4, y: 4, z: 8 (z_hi: 4, z_lo: 2; z = z_hi * 2 + z_lo), core: 2. Of those that a mesh axis runs over, the one named last changes fastest.
Arguments:
- pair: bfloat16 [768, 768, 128], P('rows', 'cols'), may hold values from -6 to 6
- token_mask: int32 [768], P('cols'), may hold values from 0 to 1
- norm_gain: float32 [128], replicated, may hold values from 0.25 to 1.75
- norm_shift: float32 [128], replicated, may hold values from -3 to 3
- in_weight: bfloat16 [128, 512], replicated, may hold values from -1.5 to 1.5
- gate_bias: float32 [128], replicated, may hold values from -4 to 4
- bias_weight: bfloat16 [128, 4], replicated, may hold values from -16 to 16
- out_weight: bfloat16 [128, 128], replicated, may hold values from -1.5 to 1.5
- out_bias: float32 [128], replicated, may hold values from -1.8 to 1.8
Outputs:
- updated: bfloat16 [768, 768, 128], P('rows', 'cols')
All inputs are finite; a program needn't handle non-finite values.
Results may differ from a plain program's by a relative error of at most 0.006.
The roundings to bfloat16 on the way count: a program that leaves them out, or rounds other values in their place, can miss the bound.
Values may be sent and summed in bfloat16 or wider, within the bound.
A program may use at most 128 MiB of HBM per device.

v0:
```python
import jax
import jax.numpy as jnp
from jax import lax
from jax.sharding import PartitionSpec as P


def broadcast(x, axis, root):
    mine = lax.axis_index(axis) == root
    return lax.psum(jnp.where(mine, x, jnp.zeros_like(x)), axis)


def layer_norm(pair_block, norm_gain, norm_shift):
    as_float = pair_block.astype(jnp.float32)
    center = jnp.mean(as_float, axis=-1, keepdims=True)
    spread = jnp.mean(jnp.square(as_float - center), axis=-1, keepdims=True)
    return ((as_float - center) * lax.rsqrt(spread + 1e-05) * norm_gain + norm_shift).astype(
        jnp.bfloat16
    )


def shards(
    pair, token_mask, norm_gain, norm_shift, in_weight, gate_bias, bias_weight, out_weight, out_bias
):
    row_count, col_count, channels = pair.shape
    head_count = bias_weight.shape[1]
    inner_width = out_weight.shape[0]
    head_size = inner_width // head_count
    normed = layer_norm(pair, norm_gain, norm_shift)
    flat_normed = normed.reshape(row_count * col_count, channels)
    bias_tile = jnp.einsum(
        "jkc,ch->jhk", normed, bias_weight, preferred_element_type=jnp.float32
    ).astype(jnp.bfloat16)
    bias_rows_all = lax.all_gather(bias_tile, "cols", axis=2, tiled=True)
    groups = lax.axis_size("rows") // lax.axis_size("cols")
    first_root = lax.axis_index("cols") * groups
    pieces = []
    for offset in range(groups):
        pieces.append(broadcast(bias_rows_all, "rows", first_root + offset))
    own_bias = jnp.concatenate(pieces, axis=0)
    query_gate = jnp.concatenate(
        (in_weight[:, :inner_width], in_weight[:, 3 * inner_width :]), axis=1
    )
    projected = jnp.dot(flat_normed, query_gate, preferred_element_type=jnp.float32)
    queries = (projected[:, :inner_width] * head_size ** (-0.5)).astype(jnp.bfloat16)
    queries = queries.reshape(row_count, col_count, head_count, head_size)
    gates = jax.nn.sigmoid(projected[:, inner_width:] + gate_bias)
    key_value_weight = in_weight[:, inner_width : 3 * inner_width]
    mask_row = token_mask.reshape(1, col_count)
    start_state = (
        jnp.full((row_count, col_count, head_count), -jnp.inf, jnp.float32),
        jnp.zeros((row_count, col_count, head_count), jnp.float32),
        jnp.zeros((row_count, col_count, inner_width), jnp.float32),
    )
    key_values = jnp.dot(flat_normed, key_value_weight, preferred_element_type=jnp.float32).astype(
        jnp.bfloat16
    )
    key_values = key_values.reshape(row_count, col_count, 2 * inner_width)
    pair_keys = lax.all_gather(key_values, "cols", axis=1, tiled=True)
    mask_in = lax.all_gather(mask_row, "cols", axis=1, tiled=True)
    state_now = start_state
    begin_at = jnp.int32(0)
    span_len = pair_keys.shape[1]
    for low_edge in range(0, span_len, col_count):
        high_edge = min(low_edge + col_count, span_len)
        attend_pair_keys = pair_keys[:, low_edge:high_edge]
        attend_begin_at = begin_at + low_edge
        attend_running_max, attend_totals, attend_summed = state_now
        attend_span_len = attend_pair_keys.shape[1]
        key_part = attend_pair_keys[..., :inner_width].reshape(
            row_count, attend_span_len, head_count, head_size
        )
        value_part = attend_pair_keys[..., inner_width:].reshape(
            row_count, attend_span_len, head_count, head_size
        )
        scores = jnp.einsum(
            "rjhd,rkhd->rjhk", queries, key_part, preferred_element_type=jnp.float32
        )
        bias_part = lax.dynamic_slice_in_dim(own_bias, attend_begin_at, attend_span_len, 2).astype(
            jnp.float32
        )
        masking = 1000000000.0 * (mask_in[:, low_edge:high_edge][0].astype(jnp.float32) - 1.0)
        scores = scores + bias_part + masking
        new_max = jnp.maximum(attend_running_max, jnp.max(scores, axis=-1))
        shrink = jnp.exp(attend_running_max - new_max)
        weights = jnp.exp(scores - new_max[..., None])
        attend_totals = attend_totals * shrink + jnp.sum(weights, axis=-1)
        mixed_part = jnp.einsum(
            "rjhk,rkhd->rjhd",
            weights.astype(jnp.bfloat16),
            value_part,
            preferred_element_type=jnp.float32,
        )
        attend_summed = (
            attend_summed.reshape(row_count, col_count, head_count, head_size) * shrink[..., None]
            + mixed_part
        )
        state_now = (
            new_max,
            attend_totals,
            attend_summed.reshape(row_count, col_count, inner_width),
        )
    running_max, totals, summed = state_now
    attended = summed.reshape(row_count, col_count, head_count, head_size) / totals[..., None]
    gated = gates.reshape(row_count, col_count, head_count, head_size) * attended
    gated = gated.astype(jnp.bfloat16).reshape(row_count * col_count, inner_width)
    updated = jnp.dot(gated, out_weight, preferred_element_type=jnp.float32) + out_bias
    return updated.astype(jnp.bfloat16).reshape(row_count, col_count, channels)


def solution(mesh):
    placed = (P("rows", "cols", None), P("cols"), P(), P(), P(), P(), P(), P(), P())
    return jax.shard_map(
        shards, mesh=mesh, in_specs=placed, out_specs=P("rows", "cols", None), check_vma=False
    )
```

profile of v0, /device:TPU:2, one launch (start us, length us, event | category | flops | bytes accessed | tf_op | source)
XLA Modules:
  0.0 610.0 jit_solution(3657278403841043322)
XLA Ops:
  13.8 30.4 %all_gather.10 = bf16[24,4,768]{0,1,2:T(4,128)(2,1)S(1)} all-gather(bf16[24,4,96]{0,1,2:T(4,128)(2,1)S(1)} %copy.144), channel_id=1, replica_groups=mesh['rows'=32,'cols'=8] {'cols'}, dimensions={2}, use_global_device_ids=true | all-gather | bytes 165888 | tf_op jit(solution)/shard_map/all_gather | solution.py:33
  51.0 10.0 %all-reduce = s32[768]{0:T(1024)S(1)} all-reduce(s32[768]{0:T(1024)S(1)} %dynamic-update-slice), channel_id=2, replica_groups=mesh['rows'=32,'cols'=8] {'cols'}, use_global_device_ids=true, to_apply=%add | all-reduce | flops 768 | bytes 6144
  62.4 2.4 reshape.407
  64.9 406.6 %all-reduce.4.cloned.1.call-done = (bf16[24,4,768]{2,0,1:T(8,128)(2,1)}, bf16[24,4,768]{2,0,1:T(8,128)(2,1)}, bf16[24,4,768]{2,0,1:T(8,128)(2,1)}, bf16[24,4,768]{2,0,1:T(8,128)(2,1)}) async-done(((bf16[24,4,768]{2,0,1:T(8,128)(2,1)}, bf16[24,4,768]{2,0,1:T(8,128)(2,1)}, bf16[24,4,768]{2,0,1:T(8,128)(2,1)}, bf16[24,4,768]{2,0,1:T(8,128)(2,1)}), (bf16[24,4,768]{2,0,1:T(8,128)(2,1)}, ...) | async-done | bytes 589840 | tf_op jit(solution)/shard_map/psum | solution.py:9
  484.6 7.4 %fusion.145 = (bf16[24,96,128]{2,1,0:T(8,128)(2,1)}, bf16[24,96,128]{2,1,0:T(8,128)(2,1)}, bf16[24,96,128]{2,1,0:T(8,128)(2,1)S(1)}, bf16[24,96,128]{2,1,0:T(8,1...) fusion(bf16[24,768,256]{2,1,0:T(8,128)(2,1)} %all-gather.3.clon, ...), kind=kLoop, calls=%fused_computation.201 | loop fusion | bytes 18874368 | tf_op jit(solution)/shard_map/slice | solution.py:72
  492.0 2.2 copy.167
  494.2 2.3 copy.162
  505.4 2.2 copy.177
  510.3 4.6 fusion.29
  514.9 3.5 fusion.28
  518.4 3.4 fusion.27
  525.1 3.5 fusion.30
  528.6 3.5 fusion.31
  532.1 3.4 fusion.32
  536.2 4.2 fusion.8
  544.5 4.7 fusion.43
  549.2 6.5 %fusion.12 = (f32[24,96,4]{1,2,0:T(4,128)}, f32[24,96,4]{1,2,0:T(4,128)}) fusion(f32[24,4,96,96]{3,2,1,0:T(8,128)} %get-tuple-element.76, f32[24,96,4]{1,2,0:T(4,128)S(1)} %bitcast.267, f32[96]{0:T(128)S(1)} %get-tuple-element.63, f32[96,4,96]{0,2,1:T(8,128)S(1)} %copy-done.19, f32[24,96,4]{1,2,0:T(4,128)S(1)} %bitcast.263, f32[96]{0:T(128)S(1)} %get-tuple-element.62, ...), kind=kLoop, calls=%fused_computation.28 | loop fusion | flops 7059456 | bytes 7521024 | tf_op jit(solution)/shard_map/reduce_sum | solution.py:86
  555.7 2.3 fusion.41
  560.9 4.8 fusion.39
  565.7 6.7 %fusion.16 = (f32[24,96,4]{1,2,0:T(4,128)}, f32[24,96,4]{1,2,0:T(4,128)}) fusion(f32[24,4,96,96]{3,2,1,0:T(8,128)} %get-tuple-element.72, f32[24,96,4]{1,2,0:T(4,128)S(1)} %bitcast.261, f32[96]{0:T(128)S(1)} %get-tuple-element.61, f32[96,4,96]{0,2,1:T(8,128)S(1)} %copy-done.13, f32[24,96,4]{1,2,0:T(4,128)S(1)} %bitcast.257, f32[96]{0:T(128)S(1)} %get-tuple-element.60, ...), kind=kLoop, calls=%fused_computation.32 | loop fusion | flops 7059456 | bytes 7521024 | tf_op jit(solution)/shard_map/reduce_sum | solution.py:86
  572.4 2.3 fusion.37
  577.6 4.7 fusion.35
  582.2 6.3 %fusion.20 = (f32[24,96,4]{1,2,0:T(4,128)}, f32[24,96,4]{1,2,0:T(4,128)}) fusion(f32[24,4,96,96]{3,2,1,0:T(8,128)} %get-tuple-element.68, f32[24,96,4]{1,2,0:T(4,128)S(1)} %bitcast.255, f32[96]{0:T(128)S(1)} %get-tuple-element.59, f32[96,4,96]{0,2,1:T(8,128)S(1)} %copy-done.12, f32[24,96,4]{1,2,0:T(4,128)S(1)} %bitcast.251, f32[96]{0:T(128)S(1)} %get-tuple-element.58, ...), kind=kLoop, calls=%fused_computation.36 | loop fusion | flops 7059456 | bytes 7521024 | tf_op jit(solution)/shard_map/reduce_sum | solution.py:86
  592.5 7.6 %fusion.75 = bf16[24,96,4,32]{1,3,2,0:T(8,128)(2,1)S(1)} fusion(f32[24,4,32,96]{3,2,1,0:T(8,128)} %fusion.33, f32[24,4,32,96]{3,2,1,0:T(8,128)} %fusion.35, f32[24,4,32,96]{3,2,1,0:T(8,128)} %fusion.37, f32[24,4,32,96]{3,2,1,0:T(8,128)} %fusion.39, f32[24,4,32,96]{3,2,1,0:T(8,128)} %fusion.41, f32[24,4,32,96]{3,2,1,0:T(8,128)} %fusion.43, ...), kind=kOutput, calls=%fused_computation.86 | convolution fusion | flops 65470464 | bytes 14672256 | tf_op jit(solution)/shard_map/rjhk,rkhd->rjhd/dot_general | solution.py:87
  (150 shorter events, 58.3 us)
Async XLA Ops:
  7.4 593.8 %copy-start = (bf16[128,128]{1,0:T(8,128)(2,1)S(1)}, bf16[128,128]{1,0:T(8,128)(2,1)}, u32[]{:S(2)}) copy-start(bf16[128,128]{1,0:T(8,128)(2,1)} %param.16) | copy-start | bytes 98308
  7.4 38.2 %copy-start.32 = (bf16[128,512]{1,0:T(8,128)(2,1)S(1)}, bf16[128,512]{1,0:T(8,128)(2,1)}, u32[]{:S(2)}) copy-start(bf16[128,512]{1,0:T(8,128)(2,1)} %param.13) | copy-start | bytes 393220
  7.4 464.1 %all-reduce.4.cloned.1.call-start = ((), (), s32[]{:S(2)}) async-start(), calls=%async_computation.1 | async-start | bytes 1179648 | tf_op jit(solution)/shard_map/psum | solution.py:9
  13.6 34.0 %copy-start.33 = (f32[128]{0:T(128)S(1)}, f32[128]{0:T(128)}, u32[]{:S(2)}) copy-start(f32[128]{0:T(128)} %param.14) | copy-start | bytes 1540
  45.5 439.0 %all-gather.3.cloned.1.call-start = ((), (), s32[]{:S(2)}) async-start(), calls=%async_computation | async-start | bytes 10616832 | tf_op jit(solution)/shard_map/all_gather | solution.py:58
  510.3 4.6 copy-start.8
  523.2 13.0 %copy-start.1 = (f32[24,4,96,96]{3,2,1,0:T(8,128)}, f32[24,4,96,96]{3,2,1,0:T(8,128)S(1)}, u32[]{:S(2)}) copy-start(f32[24,4,96,96]{3,2,1,0:T(8,128)S(1)} %get-tuple-element.78) | copy-start | bytes 10616836
  544.4 4.8 copy-start.17
  544.4 4.8 copy-start.19
  544.4 4.8 copy-start.27
  544.4 4.8 copy-start.29
  544.5 11.2 %slice-start.4 = ((s8[4718592]{0:T(1024)(128)(4,1)}), s8[4194304]{0:T(1024)(128)(4,1)S(1)}, s32[]{:S(2)}) async-start(s8[4718592]{0:T(1024)(128)(4,1)} %bitcast.229), calls=%async_computation.6 | async-start | bytes 8388608
  549.2 6.5 %slice-start.5 = ((s8[4718592]{0:T(1024)(128)(4,1)}), s8[524288]{0:T(1024)(128)(4,1)S(1)}, s32[]{:S(2)}) async-start(s8[4718592]{0:T(1024)(128)(4,1)} %bitcast.229), calls=%async_computation.7 | async-start | bytes 1048576
  560.8 4.8 copy-start.13
  560.9 4.8 copy-start.15
  560.9 4.8 copy-start.23
  560.9 4.8 copy-start.25
  560.9 11.5 %slice-start.2 = ((s8[4718592]{0:T(1024)(128)(4,1)}), s8[4194304]{0:T(1024)(128)(4,1)S(1)}, s32[]{:S(2)}) async-start(s8[4718592]{0:T(1024)(128)(4,1)} %bitcast.227), calls=%async_computation.4 | async-start | bytes 8388608
  565.7 6.7 %slice-start.3 = ((s8[4718592]{0:T(1024)(128)(4,1)}), s8[524288]{0:T(1024)(128)(4,1)S(1)}, s32[]{:S(2)}) async-start(s8[4718592]{0:T(1024)(128)(4,1)} %bitcast.227), calls=%async_computation.5 | async-start | bytes 1048576
  577.5 4.7 copy-start.10
  577.5 4.7 copy-start.12
  577.5 11.1 %slice-start = ((s8[4718592]{0:T(1024)(128)(4,1)}), s8[4194304]{0:T(1024)(128)(4,1)S(1)}, s32[]{:S(2)}) async-start(s8[4718592]{0:T(1024)(128)(4,1)} %bitcast.225), calls=%async_computation.2 | async-start | bytes 8388608
  582.2 6.4 %slice-start.1 = ((s8[4718592]{0:T(1024)(128)(4,1)}), s8[524288]{0:T(1024)(128)(4,1)S(1)}, s32[]{:S(2)}) async-start(s8[4718592]{0:T(1024)(128)(4,1)} %bitcast.225), calls=%async_computation.3 | async-start | bytes 1048576
  592.5 8.7 %copy-start.34 = (f32[128]{0:T(128)S(1)}, f32[128]{0:T(128)}, u32[]{:S(2)}) copy-start(f32[128]{0:T(128)} %param.17) | copy-start | bytes 1540
  (21 other events, 61.9 us)
Sparse Core Ops, SparseCore 0:
  45.7 425.7 all-reduce.3
Sparse Core Ops, SparseCore 1:
  47.8 195.4 all-gather.2
where the time goes:
time: 617 us; the launch traced here: 610 us
  waiting for transfers between devices  407 us (66%)
  matrix products  59.2 us (10%)
  local copies, waits for them, and re-layouts  54.4 us (9%)
  blocking collectives  40.4 us (7%)
  other arithmetic  32.8 us (5%)
  between operations  16.5 us (3%)
    psum x1, waiting for transfers between devices, broadcast(): return lax.psum(jnp.where(mine, x, jnp.zeros_like(x)), axis)  407 us
    dot_general x8, matrix products, shards(): jnp.einsum('rjhk,rkhd->rjhd', weights.astype(jnp.bfloat16), value_part, p...  30.7 us
    all_gather x1, blocking collectives, shards(): bias_rows_all = lax.all_gather(bias_tile, 'cols', axis=2, tiled=True)  30.4 us
    dot_general x8, matrix products, shards(): jnp.einsum('rjhd,rkhd->rjhk', queries, key_part, preferred_element_type=j...  24.3 us
    reduce_sum x4, other arithmetic, shards(): attend_totals = attend_totals * shrink + jnp.sum(weights, axis=-1)  23.7 us
    slice x8, local copies, waits for them, and re-layouts, shards(): attend_pair_keys[..., :inner_width]  16.8 us
    slice x9, local copies, waits for them, and re-layouts, shards(): attend_pair_keys[..., inner_width:]  16.8 us
  transfers between devices with their start and end apart: 2, of which 1 were waited for; matrix products, arithmetic and copies ran while one was open for 4% of the time, Pallas kernels for 0%

commit v1 on v0

--- a/solution.py
+++ b/solution.py
@@ -30,7 +30,16 @@
     bias_tile = jnp.einsum(
         "jkc,ch->jhk", normed, bias_weight, preferred_element_type=jnp.float32
     ).astype(jnp.bfloat16)
-    bias_rows_all = lax.all_gather(bias_tile, "cols", axis=2, tiled=True)
+    solve_sums_all_for = lambda along_axis, own_rows: jnp.concatenate(
+        lax.all_to_all(
+            jnp.stack([own_rows for _ in range(lax.axis_size(along_axis))], axis=0),
+            along_axis,
+            0,
+            0,
+        ),
+        axis=2,
+    )
+    bias_rows_all = solve_sums_all_for("cols", bias_tile)
     groups = lax.axis_size("rows") // lax.axis_size("cols")
     first_root = lax.axis_index("cols") * groups
     pieces = []

time: 617 us -> 600 us (0.972)
  blocking collectives: 40.4 us -> 9.74 us
  starting transfers between devices: 0.05 us -> 6.23 us
    all_gather x1 -> x0, blocking collectives: 30.4 us -> none  [shards(): bias_rows_all = lax.all_gather(bias_tile, 'cols', axis=2, tiled=True)]
    all_to_all x0 -> x1, starting transfers between devices: none -> 6.18 us  [shards(): lax.all_to_all(jnp.stack([own_rows for _ in range(lax.axis_size(along_axi...]
  transfers between devices with their start and end apart: 2 -> 3, of which waited for: 1 -> 2; matrix products, arithmetic and copies ran while one was open for 4% -> 4% of each run, Pallas kernels for 0% -> 0%
where the time goes in v1:
time: 600 us; the launch traced here: 592 us
  waiting for transfers between devices  411 us (68%)
  matrix products  59.3 us (10%)
  local copies, waits for them, and re-layouts  57.9 us (10%)
  other arithmetic  32 us (5%)
  between operations  16.4 us (3%)
  blocking collectives  9.74 us (2%)
  starting transfers between devices  6.23 us (1%)
    psum x1, waiting for transfers between devices, broadcast(): return lax.psum(jnp.where(mine, x, jnp.zeros_like(x)), axis)  406 us
    dot_general x8, matrix products, shards(): jnp.einsum('rjhk,rkhd->rjhd', weights.astype(jnp.bfloat16), value_part, p...  30.7 us
    dot_general x8, matrix products, shards(): jnp.einsum('rjhd,rkhd->rjhk', queries, key_part, preferred_element_type=j...  24.4 us
    reduce_sum x4, other arithmetic, shards(): attend_totals = attend_totals * shrink + jnp.sum(weights, axis=-1)  23.7 us
    slice x9, local copies, waits for them, and re-layouts, shards(): attend_pair_keys[..., inner_width:]  16.8 us
    slice x8, local copies, waits for them, and re-layouts, shards(): attend_pair_keys[..., :inner_width]  16.8 us
  transfers between devices with their start and end apart: 3, of which 2 were waited for; matrix products, arithmetic and copies ran while one was open for 4% of the time, Pallas kernels for 0%

profile of v1, /device:TPU:2, one launch (start us, length us, event | category | flops | bytes accessed | tf_op | source)
XLA Modules:
  0.0 592.5 jit_solution(15681417198937394604)
XLA Ops:
  14.3 6.2 %all-to-all-start = ((bf16[8,24,4,96]{3,1,2,0:T(8,128)(2,1)}), bf16[8,24,4,96]{3,1,2,0:T(8,128)(2,1)S(1)}, u32[]{:S(2)}, u32[]{:S(2)}) async-start(bf16[8,24,4,96]{3,1,2,0:T(8,128)(2,1)} %stack.2), calls=%async_computation | async-start | bytes 393216 | tf_op jit(solution)/shard_map/all_to_all | solution.py:34
  20.5 5.2 all-to-all-done
  34.9 9.7 %all-reduce = s32[768]{0:T(1024)S(1)} all-reduce(s32[768]{0:T(1024)S(1)} %dynamic-update-slice), channel_id=2, replica_groups=mesh['rows'=32,'cols'=8] {'cols'}, use_global_device_ids=true, to_apply=%add | all-reduce | flops 768 | bytes 6144
  46.0 2.3 reshape.423
  48.4 405.6 %all-reduce.4.cloned.1.call-done = (bf16[24,4,768]{2,0,1:T(8,128)(2,1)}, bf16[24,4,768]{2,0,1:T(8,128)(2,1)}, bf16[24,4,768]{2,0,1:T(8,128)(2,1)}, bf16[24,4,768]{2,0,1:T(8,128)(2,1)}) async-done(((bf16[24,4,768]{2,0,1:T(8,128)(2,1)}, bf16[24,4,768]{2,0,1:T(8,128)(2,1)}, bf16[24,4,768]{2,0,1:T(8,128)(2,1)}, bf16[24,4,768]{2,0,1:T(8,128)(2,1)}), (bf16[24,4,768]{2,0,1:T(8,128)(2,1)}, ...) | async-done | bytes 589840 | tf_op jit(solution)/shard_map/psum | solution.py:9
  467.1 7.4 %fusion.145 = (bf16[24,96,128]{2,1,0:T(8,128)(2,1)}, bf16[24,96,128]{2,1,0:T(8,128)(2,1)}, bf16[24,96,128]{2,1,0:T(8,128)(2,1)S(1)}, bf16[24,96,128]{2,1,0:T(8,1...) fusion(bf16[24,768,256]{2,1,0:T(8,128)(2,1)} %all-gather.3.clon, ...), kind=kLoop, calls=%fused_computation.201 | loop fusion | bytes 18874368 | tf_op jit(solution)/shard_map/slice | solution.py:81
  476.7 2.2 copy.140
  487.8 2.2 copy.155
  492.7 4.6 fusion.29
  497.4 3.5 fusion.28
  500.9 3.4 fusion.27
  507.5 3.4 fusion.30
  511.0 3.5 fusion.31
  514.5 3.4 fusion.32
  518.6 4.2 fusion.8
  526.9 4.7 fusion.43
  531.7 6.5 %fusion.12 = (f32[24,96,4]{1,2,0:T(4,128)}, f32[24,96,4]{1,2,0:T(4,128)}) fusion(f32[24,4,96,96]{3,2,1,0:T(8,128)} %get-tuple-element.76, f32[24,96,4]{1,2,0:T(4,128)S(1)} %bitcast.291, f32[96]{0:T(128)S(1)} %get-tuple-element.63, f32[96,4,96]{0,2,1:T(8,128)S(1)} %copy-done.19, f32[24,96,4]{1,2,0:T(4,128)S(1)} %bitcast.287, f32[96]{0:T(128)S(1)} %get-tuple-element.62, ...), kind=kLoop, calls=%fused_computation.28 | loop fusion | flops 7059456 | bytes 7521024 | tf_op jit(solution)/shard_map/reduce_sum | solution.py:95
  538.1 2.3 fusion.41
  543.3 4.8 fusion.39
  548.1 6.7 %fusion.16 = (f32[24,96,4]{1,2,0:T(4,128)}, f32[24,96,4]{1,2,0:T(4,128)}) fusion(f32[24,4,96,96]{3,2,1,0:T(8,128)} %get-tuple-element.72, f32[24,96,4]{1,2,0:T(4,128)S(1)} %bitcast.285, f32[96]{0:T(128)S(1)} %get-tuple-element.61, f32[96,4,96]{0,2,1:T(8,128)S(1)} %copy-done.13, f32[24,96,4]{1,2,0:T(4,128)S(1)} %bitcast.281, f32[96]{0:T(128)S(1)} %get-tuple-element.60, ...), kind=kLoop, calls=%fused_computation.32 | loop fusion | flops 7059456 | bytes 7521024 | tf_op jit(solution)/shard_map/reduce_sum | solution.py:95
  554.8 2.3 fusion.37
  560.0 4.7 fusion.35
  564.7 6.3 %fusion.20 = (f32[24,96,4]{1,2,0:T(4,128)}, f32[24,96,4]{1,2,0:T(4,128)}) fusion(f32[24,4,96,96]{3,2,1,0:T(8,128)} %get-tuple-element.68, f32[24,96,4]{1,2,0:T(4,128)S(1)} %bitcast.279, f32[96]{0:T(128)S(1)} %get-tuple-element.59, f32[96,4,96]{0,2,1:T(8,128)S(1)} %copy-done.12, f32[24,96,4]{1,2,0:T(4,128)S(1)} %bitcast.275, f32[96]{0:T(128)S(1)} %get-tuple-element.58, ...), kind=kLoop, calls=%fused_computation.36 | loop fusion | flops 7059456 | bytes 7521024 | tf_op jit(solution)/shard_map/reduce_sum | solution.py:95
  574.9 7.6 %fusion.75 = bf16[24,96,4,32]{1,3,2,0:T(8,128)(2,1)S(1)} fusion(f32[24,4,32,96]{3,2,1,0:T(8,128)} %fusion.33, f32[24,4,32,96]{3,2,1,0:T(8,128)} %fusion.35, f32[24,4,32,96]{3,2,1,0:T(8,128)} %fusion.37, f32[24,4,32,96]{3,2,1,0:T(8,128)} %fusion.39, f32[24,4,32,96]{3,2,1,0:T(8,128)} %fusion.41, f32[24,4,32,96]{3,2,1,0:T(8,128)} %fusion.43, ...), kind=kOutput, calls=%fused_computation.86 | convolution fusion | flops 65470464 | bytes 14672256 | tf_op jit(solution)/shard_map/rjhk,rkhd->rjhd/dot_general | solution.py:96
  (159 shorter events, 63.4 us)
Async XLA Ops:
  7.4 576.3 %copy-start = (bf16[128,128]{1,0:T(8,128)(2,1)S(1)}, bf16[128,128]{1,0:T(8,128)(2,1)}, u32[]{:S(2)}) copy-start(bf16[128,128]{1,0:T(8,128)(2,1)} %param.16) | copy-start | bytes 98308
  7.4 22.2 %copy-start.32 = (bf16[128,512]{1,0:T(8,128)(2,1)S(1)}, bf16[128,512]{1,0:T(8,128)(2,1)}, u32[]{:S(2)}) copy-start(bf16[128,512]{1,0:T(8,128)(2,1)} %param.13) | copy-start | bytes 393220
  14.3 11.4 %all-to-all-start = ((bf16[8,24,4,96]{3,1,2,0:T(8,128)(2,1)}), bf16[8,24,4,96]{3,1,2,0:T(8,128)(2,1)S(1)}, u32[]{:S(2)}, u32[]{:S(2)}) async-start(bf16[8,24,4,96]{3,1,2,0:T(8,128)(2,1)} %stack.2), calls=%async_computation | async-start | bytes 393216 | tf_op jit(solution)/shard_map/all_to_all | solution.py:34
  20.5 433.5 %all-reduce.4.cloned.1.call-start = ((), (), s32[]{:S(2)}) async-start(), calls=%async_computation.2 | async-start | bytes 1179648 | tf_op jit(solution)/shard_map/psum | solution.py:9
  25.9 5.7 copy-start.33
  29.5 437.5 %all-gather.3.cloned.1.call-start = ((), (), s32[]{:S(2)}) async-start(), calls=%async_computation.1 | async-start | bytes 10616832 | tf_op jit(solution)/shard_map/all_gather | solution.py:67
  505.6 13.0 %copy-start.1 = (f32[24,4,96,96]{3,2,1,0:T(8,128)}, f32[24,4,96,96]{3,2,1,0:T(8,128)S(1)}, u32[]{:S(2)}) copy-start(f32[24,4,96,96]{3,2,1,0:T(8,128)S(1)} %get-tuple-element.78) | copy-start | bytes 10616836
  526.9 4.8 copy-start.17
  526.9 4.8 copy-start.19
  526.9 4.7 copy-start.27
  526.9 4.7 copy-start.29
  526.9 11.2 %slice-start.4 = ((s8[4718592]{0:T(1024)(128)(4,1)}), s8[4194304]{0:T(1024)(128)(4,1)S(1)}, s32[]{:S(2)}) async-start(s8[4718592]{0:T(1024)(128)(4,1)} %bitcast.253), calls=%async_computation.7 | async-start | bytes 8388608
  531.6 6.5 %slice-start.5 = ((s8[4718592]{0:T(1024)(128)(4,1)}), s8[524288]{0:T(1024)(128)(4,1)S(1)}, s32[]{:S(2)}) async-start(s8[4718592]{0:T(1024)(128)(4,1)} %bitcast.253), calls=%async_computation.8 | async-start | bytes 1048576
  543.3 4.8 copy-start.13
  543.3 4.8 copy-start.15
  543.3 4.8 copy-start.23
  543.3 4.8 copy-start.25
  543.3 11.5 %slice-start.2 = ((s8[4718592]{0:T(1024)(128)(4,1)}), s8[4194304]{0:T(1024)(128)(4,1)S(1)}, s32[]{:S(2)}) async-start(s8[4718592]{0:T(1024)(128)(4,1)} %bitcast.251), calls=%async_computation.5 | async-start | bytes 8388608
  548.1 6.7 %slice-start.3 = ((s8[4718592]{0:T(1024)(128)(4,1)}), s8[524288]{0:T(1024)(128)(4,1)S(1)}, s32[]{:S(2)}) async-start(s8[4718592]{0:T(1024)(128)(4,1)} %bitcast.251), calls=%async_computation.6 | async-start | bytes 1048576
  560.0 4.7 copy-start.10
  560.0 4.7 copy-start.12
  560.0 11.1 %slice-start = ((s8[4718592]{0:T(1024)(128)(4,1)}), s8[4194304]{0:T(1024)(128)(4,1)S(1)}, s32[]{:S(2)}) async-start(s8[4718592]{0:T(1024)(128)(4,1)} %bitcast.249), calls=%async_computation.3 | async-start | bytes 8388608
  564.7 6.4 %slice-start.1 = ((s8[4718592]{0:T(1024)(128)(4,1)}), s8[524288]{0:T(1024)(128)(4,1)S(1)}, s32[]{:S(2)}) async-start(s8[4718592]{0:T(1024)(128)(4,1)} %bitcast.249), calls=%async_computation.4 | async-start | bytes 1048576
  574.9 8.7 %copy-start.34 = (f32[128]{0:T(128)S(1)}, f32[128]{0:T(128)}, u32[]{:S(2)}) copy-start(f32[128]{0:T(128)} %param.17) | copy-start | bytes 1540
  (22 other events, 66.4 us)
Sparse Core Ops, SparseCore 0:
  29.6 424.2 all-reduce.3
Sparse Core Ops, SparseCore 1:
  31.8 193.9 all-gather.2
